TPU v7x, 256 devices: a whole 4x4x8 slice. The times are simulated.
256 devices in a mesh: wire: 64 (over z, y, core), col: 4 (over x).
Axes of the slice: x: 4, y: 4, z: 8, core: 2. Of those that a mesh axis runs over, the one named last changes fastest.
Arguments:
- search: float32 [196608, 384], P('wire', 'col')
- block_values: float32 [196608, 256], P('wire'), may hold values from -0.375 to 0.375
- block_cols: int32 [3072, 4], P('wire'), may hold values from 0 to 3071, as said below
- ritz: float32 [384, 128], replicated, may hold values from -0.3125 to 0.3125
Outputs:
- new_modes: float32 [196608, 128], P('wire', 'col')
- residual: float32 [196608, 128], P('wire', 'col')
- theta: float32 [128], P('col')
- gram_stiff: float32 [384, 384], P(None, 'col')
- gram_mass: float32 [384, 384], P(None, 'col')
Inputs may be any that keep to these rules, and one draw needn't show every extreme that they name: Block rows are in groups of 48, b in group g = b // 48. block_cols[b, 0] = b. Column 1 names a block row of group g. For even b, column 2 names a block row of group g + 1 and column 3 one of group g + 2; for odd b, groups g - 1 and g - 2; groups counted around the loop of all groups.
All inputs are finite; a program needn't handle non-finite values.
Results may differ from a plain program's by a relative error of at most 0.0003.
Values sent between devices are 32-bit elements; how exact they have to be, the bound alone decides.
No kernel may reach another device: no remote copies, remote signals or barrier semaphores. Data moves between devices by JAX's collectives and lax.ppermute only.
A program may use at most 64 MiB of HBM per device.

v0:
```python
import jax
import jax.numpy as jnp
from jax import lax
from jax.sharding import PartitionSpec as P


def shifted(array, axis, by):
    length = lax.axis_size(axis)
    return lax.ppermute(array, axis, [(i, (i + by) % length) for i in range(length)])


def neighbour_group(search, distance):
    return shifted(search, "wire", distance)


def shards(search, block_values, block_cols, ritz):
    high = lax.Precision.HIGHEST
    rows, width = search.shape
    blk = block_cols.shape[0]
    block = rows // blk
    slots = block_cols.shape[1]
    col_here = lax.axis_index("col")
    wire_here = lax.axis_index("wire")
    wire_count = lax.axis_size("wire")
    extended = jnp.concatenate(
        [
            neighbour_group(search, 2),
            neighbour_group(search, 1),
            search,
            neighbour_group(search, -1),
            neighbour_group(search, -2),
        ],
        axis=0,
    )
    ext_blocks = extended.reshape(5 * blk, block, width)
    owner = block_cols // blk
    offset = (owner - wire_here + 2 + wire_count) % wire_count
    local_index = offset * blk + block_cols % blk
    picked = ext_blocks[local_index].reshape(blk, slots * block, width)
    values = block_values.reshape(blk, block, slots * block)
    product = jnp.einsum("bik,bkc->bic", values, picked, precision=high).reshape(rows, width)
    image = 4.0 * search + product
    paired = jnp.concatenate([image, search], axis=1)
    partial_gram = jnp.einsum(
        "rk,rc->kc", lax.all_gather(search, "col", axis=1, tiled=True), paired, precision=high
    )
    mine = lax.dynamic_slice_in_dim(ritz, col_here * width, width, 0)
    modes_part = jnp.dot(search, mine, precision=high, preferred_element_type=jnp.float32)
    image_part = jnp.dot(image, mine, precision=high, preferred_element_type=jnp.float32)
    new_modes, new_image = (
        lax.psum_scatter(modes_part, "col", scatter_dimension=1, tiled=True),
        lax.psum_scatter(image_part, "col", scatter_dimension=1, tiled=True),
    )
    total_rows = jnp.float32(rows * wire_count)
    gram_total = lax.psum(partial_gram, "wire") / total_rows
    gram_stiff = gram_total[:, :width]
    gram_mass = gram_total[:, width:]
    mine_rows = lax.dynamic_slice_in_dim(ritz, col_here * width, width, 0)
    left_stiff = jnp.einsum("ab,aj->jb", gram_stiff, ritz, precision=high)
    left_mass = jnp.einsum("ab,aj->jb", gram_mass, ritz, precision=high)
    numer_terms = jnp.sum(left_stiff * mine_rows.T, axis=1)
    denom_terms = jnp.sum(left_mass * mine_rows.T, axis=1)
    sums = lax.psum_scatter(
        jnp.stack([numer_terms, denom_terms]), "col", scatter_dimension=1, tiled=True
    )
    theta = sums[0] / sums[1]
    residual = new_image - new_modes * theta[None, :]
    return (new_modes, residual, theta, gram_stiff, gram_mass)


def solution(mesh):
    placed = (P("wire", "col"), P("wire", None), P("wire", None), P())
    return jax.shard_map(
        shards,
        mesh=mesh,
        in_specs=placed,
        out_specs=(P("wire", "col"), P("wire", "col"), P("col"), P(None, "col"), P(None, "col")),
        check_vma=False,
    )
```

profile of v0, /device:TPU:1, one launch (start us, length us, event | category | flops | bytes accessed | tf_op | source)
XLA Modules:
  0.0 370.5 jit_solution(8601047787876571192)
XLA Ops:
  8.0 2.2 collective-permute-start
  10.2 2.1 collective-permute-start.1
  12.3 5.5 %collective-permute-start.3 = (f32[3072,96]{0,1:T(8,128)}, f32[3072,96]{0,1:T(8,128)}, u32[]{:S(2)}, u32[]{:S(2)}) collective-permute-start(f32[3072,96]{0,1:T(8,128)} %param.4), channel_id=1, source_target_pairs={{0,248},{4,252},{8,0},{12,4},{16,8},{20,12},{24,16},{28,20},{32,24... | collective-permute-start | bytes 3538952 | tf_op jit(solution)/shard_map/ppermute | solution.py:9
  18.7 24.2 %collective-permute-done = f32[3072,96]{0,1:T(8,128)} collective-permute-done((f32[3072,96]{0,1:T(8,128)}, f32[3072,96]{0,1:T(8,128)}, u32[]{:S(2)}, u32[]{:S(2)}) %collective-permute-start) | collective-permute-done | bytes 1179680 | tf_op jit(solution)/shard_map/ppermute | solution.py:9
  42.9 2.4 constant_dynamic-update-slice_fusion.4
  45.2 3.7 collective-permute-done.1
  48.9 2.4 constant_dynamic-update-slice_fusion.3
  51.3 1.1 constant_dynamic-update-slice_fusion.2
  52.4 2.4 constant_dynamic-update-slice_fusion.1
  54.8 2.4 constant_dynamic-update-slice_fusion
  57.2 8.2 %copy.14 = f32[15360,96]{1,0:T(8,128)} copy(f32[15360,96]{0,1:T(8,128)} %constant_dynamic-update-slice_fusion) | data formatting | bytes 11796480 | tf_op jit(solution)/shard_map/concatenate | solution.py:25
  65.3 6.9 %gather_fusion = f32[192,64,96]{2,1,0:T(8,128)} fusion(f32[240,64,96]{2,1,0:T(8,128)} %bitcast.26, s32[1024]{0:T(1024)S(1)} %pad_clamp_fusion), kind=kCustom, calls=%fused_computation | custom fusion | bytes 9437952 | tf_op jit(solution)/shard_map/gather | solution.py:39
  72.2 7.2 %fusion.21 = f32[48,96,64]{1,2,0:T(8,128)} fusion(f32[48,256,96]{2,1,0:T(8,128)} %bitcast.27, f32[48,64,256]{2,1,0:T(8,128)S(1)} %bitcast.25), kind=kOutput, calls=%fused_computation.41 | convolution fusion | flops 905969664 | bytes 9043968 | tf_op jit(solution)/shard_map/bik,bkc->bic/dot_general | solution.py:41
  79.5 2.9 copy.17
  82.4 2.8 multiply_add_fusion
  85.2 8.7 %fusion.4 = f32[384,192]{0,1:T(8,128)} fusion(f32[3072,384]{0,1:T(8,128)} %all-gather.2.cloned.1.call-done, f32[3072,96]{0,1:T(8,128)} %param.4, f32[3072,96]{0,1:T(8,128)} %multiply_add_fusion), kind=kOutput, calls=%fused_computation.7 | convolution fusion | flops 2718498816 | bytes 7372800 | tf_op jit(solution)/shard_map/rk,rc->kc/dot_general | solution.py:44
  93.9 182.5 %all-reduce.2.cloned.1.call-done = f32[384,192]{0,1:T(8,128)} async-done(((f32[384,192]{0,1:T(8,128)}), f32[384,192]{0,1:T(8,128)}) %all-reduce.2.cloned.1.call-update) | async-done | bytes 294928 | tf_op jit(solution)/shard_map/psum | solution.py:55
  276.4 1.0 broadcast_multiply_fusion
  279.2 3.9 %convolution_bitcast_fusion = f32[3072,128]{0,1:T(8,128)} fusion(f32[3072,96]{0,1:T(8,128)} %param.4, f32[384,128]{1,0:T(8,128)S(1)} %copy-done.2, s32[]{:T(128)S(6)} %select_n.23), kind=kOutput, calls=%fused_computation.1 | convolution fusion | flops 452984832 | bytes 2801668 | tf_op jit(solution)/shard_map/dot_general | solution.py:48
  283.2 3.9 %fusion.9 = f32[3072,128]{0,1:T(8,128)} fusion(f32[3072,96]{0,1:T(8,128)} %multiply_add_fusion, f32[384,128]{1,0:T(8,128)S(1)} %copy-done.2, s32[]{:T(128)S(6)} %select_n.23), kind=kOutput, calls=%fused_computation.14 | convolution fusion | flops 452984832 | bytes 2801668 | tf_op jit(solution)/shard_map/dot_general | solution.py:49
  287.0 12.1 %reduce-scatter.10.cloned.1.call-done = f32[32,2]{1,0:T(8,128)} async-done(((f32[128,2]{1,0:T(8,128)}), f32[32,2]{1,0:T(8,128)}) %reduce-scatter.10.cloned.1.call-update) | async-done | bytes 272
  300.2 31.4 %reduce-scatter.6.cloned.1.call-done = f32[3072,32]{0,1:T(8,128)} async-done(((f32[3072,128]{0,1:T(8,128)}), f32[3072,32]{0,1:T(8,128)}) %reduce-scatter.6.cloned.1.call-update) | async-done | bytes 393232 | tf_op jit(solution)/shard_map/reduce_scatter | solution.py:51
  331.6 30.4 %reduce-scatter.8.cloned.1.call-done = f32[3072,32]{0,1:T(8,128)} async-done(((f32[3072,128]{0,1:T(8,128)}), f32[3072,32]{0,1:T(8,128)}) %reduce-scatter.8.cloned.1.call-update) | async-done | bytes 393232 | tf_op jit(solution)/shard_map/reduce_scatter | solution.py:52
  362.0 2.0 multiply_subtract_fusion
  (39 shorter events, 4.6 us)
Async XLA Ops:
  7.2 65.0 %copy-start = (f32[3072,256]{1,0:T(8,128)S(1)}, f32[3072,256]{1,0:T(8,128)}, u32[]{:S(2)}) copy-start(f32[3072,256]{1,0:T(8,128)} %param.5) | copy-start | bytes 9437188
  7.2 78.0 %all-gather.2.cloned.1.call-start = ((), (), s32[]{:S(2)}) async-start(), calls=%async_computation.5 | async-start | bytes 5898240 | tf_op jit(solution)/shard_map/all_gather | solution.py:45
  7.9 268.5 %all-reduce.2.cloned.1.call-start = ((), (), s32[]{:S(2)}) async-start(), calls=%async_computation.6 | async-start | bytes 589824 | tf_op jit(solution)/shard_map/psum | solution.py:55
  8.0 34.9 %collective-permute-start = (f32[3072,96]{0,1:T(8,128)}, f32[3072,96]{0,1:T(8,128)}, u32[]{:S(2)}, u32[]{:S(2)}) collective-permute-start(f32[3072,96]{0,1:T(8,128)} %param.4), channel_id=1, source_target_pairs={{0,8},{4,12},{8,16},{12,20},{16,24},{20,28},{24,32},{28,36},{32,40... | collective-permute-start | bytes 3538952 | tf_op jit(solution)/shard_map/ppermute | solution.py:9
  10.2 38.7 %collective-permute-start.1 = (f32[3072,96]{0,1:T(8,128)}, f32[3072,96]{0,1:T(8,128)}, u32[]{:S(2)}, u32[]{:S(2)}) collective-permute-start(f32[3072,96]{0,1:T(8,128)} %param.4), channel_id=1, source_target_pairs={{0,4},{4,8},{8,12},{12,16},{16,20},{20,24},{24,28},{28,32},{32,36}... | collective-permute-start | bytes 3538952 | tf_op jit(solution)/shard_map/ppermute | solution.py:9
  12.3 40.1 %collective-permute-start.2 = (f32[3072,96]{0,1:T(8,128)}, f32[3072,96]{0,1:T(8,128)}, u32[]{:S(2)}, u32[]{:S(2)}) collective-permute-start(f32[3072,96]{0,1:T(8,128)} %param.4), channel_id=1, source_target_pairs={{0,252},{4,0},{8,4},{12,8},{16,12},{20,16},{24,20},{28,24},{32,28}... | collective-permute-start | bytes 3538952 | tf_op jit(solution)/shard_map/ppermute | solution.py:9
  12.3 42.5 %collective-permute-start.3 = (f32[3072,96]{0,1:T(8,128)}, f32[3072,96]{0,1:T(8,128)}, u32[]{:S(2)}, u32[]{:S(2)}) collective-permute-start(f32[3072,96]{0,1:T(8,128)} %param.4), channel_id=1, source_target_pairs={{0,248},{4,252},{8,0},{12,4},{16,8},{20,12},{24,16},{28,20},{32,24... | collective-permute-start | bytes 3538952 | tf_op jit(solution)/shard_map/ppermute | solution.py:9
  18.7 32.6 %copy-start.1 = (f32[3072,96]{0,1:T(8,128)S(1)}, f32[3072,96]{0,1:T(8,128)}, u32[]{:S(2)}) copy-start(f32[3072,96]{0,1:T(8,128)} %param.4) | copy-start | bytes 3538948
  85.2 192.3 %copy-start.2 = (f32[384,128]{1,0:T(8,128)S(1)}, f32[384,128]{1,0:T(8,128)}, u32[]{:S(2)}) copy-start(f32[384,128]{1,0:T(8,128)} %param.7) | copy-start | bytes 589828
  93.9 205.3 %reduce-scatter.10.cloned.1.call-start = ((), (), s32[]{:S(2)}) async-start(), calls=%async_computation.7 | async-start | bytes 81920
  277.4 0.7 copy-start.4
  277.4 5.7 %copy-start.3 = (f32[384,96]{0,1:T(8,128)}, f32[384,96]{0,1:T(8,128)S(1)}, u32[]{:S(2)}) copy-start(f32[384,96]{0,1:T(8,128)S(1)} %get-tuple-element.5) | copy-start | bytes 442372
  279.2 52.4 %reduce-scatter.6.cloned.1.call-start = ((), (), s32[]{:S(2)}) async-start(), calls=%async_computation.3 | async-start | bytes 1966080 | tf_op jit(solution)/shard_map/reduce_scatter | solution.py:51
  283.1 78.9 %reduce-scatter.8.cloned.1.call-start = ((), (), s32[]{:S(2)}) async-start(), calls=%async_computation.4 | async-start | bytes 1966080 | tf_op jit(solution)/shard_map/reduce_scatter | solution.py:52
  300.2 63.8 %copy-start.5 = (f32[32]{0:T(128)}, f32[32]{0:T(128)S(1)}, u32[]{:S(2)}) copy-start(f32[32]{0:T(128)S(1)} %divide_bitcast_fusion) | copy-start | bytes 388
Sparse Core Ops, SparseCore 0:
  9.8 58.6 all-gather.1
  94.0 182.3 all-reduce.1
  279.5 19.6 reduce-scatter.9
  302.1 29.3 reduce-scatter.5
  334.0 28.0 reduce-scatter.7
where the time goes:
time: 371 us
  waiting for transfers between devices  285 us (77%)
  local copies, waits for them, and re-layouts  30.9 us (8%)
  matrix products  24.2 us (7%)
  between operations  13.9 us (4%)
  starting transfers between devices  9.98 us (3%)
  other arithmetic  6.48 us (2%)
    psum x1, waiting for transfers between devices, shards(): gram_total = lax.psum(partial_gram, 'wire') / total_rows  182 us
    reduce_scatter x1, waiting for transfers between devices, shards(): lax.psum_scatter(modes_part, 'col', scatter_dimension=1, tiled=True)  31.4 us
    reduce_scatter x1, waiting for transfers between devices, shards(): lax.psum_scatter(image_part, 'col', scatter_dimension=1, tiled=True)  30.4 us
    ppermute x4, waiting for transfers between devices, shifted(): lax.ppermute(array, axis, [(i, (i + by) % length) for i in range(length)])  27.9 us
    unnamed x6, waiting for transfers between devices  12.9 us
    concatenate x2, local copies, waits for them, and re-layouts, shards(): jnp.concatenate([neighbour_group(search, 2), neighbour_group(search, 1),...  10.5 us
    ppermute x4, starting transfers between devices, shifted(): lax.ppermute(array, axis, [(i, (i + by) % length) for i in range(length)])  9.78 us
    unnamed x19, local copies, waits for them, and re-layouts  9.5 us
  transfers between devices with their start and end apart: 9, of which 6 were waited for; matrix products, arithmetic and copies ran while one was open for 13% of the time, Pallas kernels for 0%

commit v1 on v0

--- a/solution.py
+++ b/solution.py
@@ -52,7 +52,7 @@
         lax.psum_scatter(image_part, "col", scatter_dimension=1, tiled=True),
     )
     total_rows = jnp.float32(rows * wire_count)
-    gram_total = lax.psum(partial_gram, "wire") / total_rows
+    gram_total = jnp.sum(lax.all_gather(partial_gram, "wire"), axis=0) / total_rows
     gram_stiff = gram_total[:, :width]
     gram_mass = gram_total[:, width:]
     mine_rows = lax.dynamic_slice_in_dim(ritz, col_here * width, width, 0)

time: 371 us -> 317 us (0.85)
  waiting for transfers between devices: 285 us -> 210 us
  local copies, waits for them, and re-layouts: 30.9 us -> 46.5 us
  other arithmetic: 6.48 us -> 13.4 us
    psum x1 -> x0, waiting for transfers between devices: 182 us -> none  [shards(): gram_total = lax.psum(partial_gram, 'wire') / total_rows]
    all_gather x0 -> x1, waiting for transfers between devices: none -> 109 us  [shards(): lax.all_gather(partial_gram, 'wire')]
    unnamed x19 -> x26, local copies, waits for them, and re-layouts: 9.5 us -> 24.9 us
    reduce_sum x0 -> x1, other arithmetic: none -> 9.32 us  [shards(): jnp.sum(lax.all_gather(partial_gram, 'wire'), axis=0) / total_rows]
  transfers between devices with their start and end apart: 9 -> 9, of which waited for: 6 -> 6; matrix products, arithmetic and copies ran while one was open for 13% -> 15% of each run, Pallas kernels for 0% -> 0%
where the time goes in v1:
time: 317 us
  waiting for transfers between devices  210 us (66%)
  local copies, waits for them, and re-layouts  46.5 us (15%)
  matrix products  22.2 us (7%)
  between operations  13.9 us (4%)
  other arithmetic  13.4 us (4%)
  starting transfers between devices  10.2 us (3%)
    all_gather x1, waiting for transfers between devices, shards(): lax.all_gather(partial_gram, 'wire')  109 us
    reduce_scatter x1, waiting for transfers between devices, shards(): lax.psum_scatter(modes_part, 'col', scatter_dimension=1, tiled=True)  31.4 us
    reduce_scatter x1, waiting for transfers between devices, shards(): lax.psum_scatter(image_part, 'col', scatter_dimension=1, tiled=True)  30.5 us
    ppermute x4, waiting for transfers between devices, shifted(): lax.ppermute(array, axis, [(i, (i + by) % length) for i in range(length)])  27.8 us
    unnamed x26, local copies, waits for them, and re-layouts  24.9 us
    unnamed x6, waiting for transfers between devices  11.5 us
    concatenate x2, local copies, waits for them, and re-layouts, shards(): jnp.concatenate([neighbour_group(search, 2), neighbour_group(search, 1),...  10.6 us
    ppermute x4, starting transfers between devices, shifted(): lax.ppermute(array, axis, [(i, (i + by) % length) for i in range(length)])  9.78 us
  transfers between devices with their start and end apart: 9, of which 6 were waited for; matrix products, arithmetic and copies ran while one was open for 15% of the time, Pallas kernels for 0%

profile of v1, /device:TPU:1, one launch (start us, length us, event | category | flops | bytes accessed | tf_op | source)
XLA Modules:
  0.0 316.6 jit_solution(13587835479338508905)
XLA Ops:
  8.0 2.2 collective-permute-start
  10.2 2.1 collective-permute-start.1
  12.3 5.5 %collective-permute-start.3 = (f32[3072,96]{0,1:T(8,128)}, f32[3072,96]{0,1:T(8,128)}, u32[]{:S(2)}, u32[]{:S(2)}) collective-permute-start(f32[3072,96]{0,1:T(8,128)} %param.4), channel_id=1, source_target_pairs={{0,248},{4,252},{8,0},{12,4},{16,8},{20,12},{24,16},{28,20},{32,24... | collective-permute-start | bytes 3538952 | tf_op jit(solution)/shard_map/ppermute | solution.py:9
  18.7 24.2 %collective-permute-done = f32[3072,96]{0,1:T(8,128)} collective-permute-done((f32[3072,96]{0,1:T(8,128)}, f32[3072,96]{0,1:T(8,128)}, u32[]{:S(2)}, u32[]{:S(2)}) %collective-permute-start) | collective-permute-done | bytes 1179680 | tf_op jit(solution)/shard_map/ppermute | solution.py:9
  42.9 2.4 constant_dynamic-update-slice_fusion.4
  45.3 3.6 %collective-permute-done.1 = f32[3072,96]{0,1:T(8,128)} collective-permute-done((f32[3072,96]{0,1:T(8,128)}, f32[3072,96]{0,1:T(8,128)}, u32[]{:S(2)}, u32[]{:S(2)}) %collective-permute-start.1) | collective-permute-done | bytes 1179680 | tf_op jit(solution)/shard_map/ppermute | solution.py:9
  48.9 2.4 constant_dynamic-update-slice_fusion.3
  52.4 2.4 constant_dynamic-update-slice_fusion.1
  54.8 2.4 constant_dynamic-update-slice_fusion
  57.2 8.2 %copy.14 = f32[15360,96]{1,0:T(8,128)} copy(f32[15360,96]{0,1:T(8,128)} %constant_dynamic-update-slice_fusion) | data formatting | bytes 11796480 | tf_op jit(solution)/shard_map/concatenate | solution.py:25
  65.4 6.9 %gather_fusion = f32[192,64,96]{2,1,0:T(8,128)} fusion(f32[240,64,96]{2,1,0:T(8,128)} %bitcast.31, s32[1024]{0:T(1024)S(1)} %pad_clamp_fusion), kind=kCustom, calls=%fused_computation | custom fusion | bytes 9437952 | tf_op jit(solution)/shard_map/gather | solution.py:39
  72.3 7.2 %fusion.21 = f32[48,96,64]{1,2,0:T(8,128)} fusion(f32[48,256,96]{2,1,0:T(8,128)} %bitcast.32, f32[48,64,256]{2,1,0:T(8,128)S(1)} %bitcast.30), kind=kOutput, calls=%fused_computation.42 | convolution fusion | flops 905969664 | bytes 9043968 | tf_op jit(solution)/shard_map/bik,bkc->bic/dot_general | solution.py:41
  79.5 3.0 copy.17
  82.5 1.4 multiply_add_fusion
  84.0 7.7 %fusion.4 = f32[384,192]{0,1:T(8,128)} fusion(f32[3072,384]{0,1:T(8,128)} %all-gather.4.cloned.1.call-done, f32[3072,96]{0,1:T(8,128)S(1)} %copy-done.3, f32[3072,96]{0,1:T(8,128)S(1)} %multiply_add_fusion), kind=kOutput, calls=%fused_computation.8 | convolution fusion | flops 2718498816 | bytes 7372800 | tf_op jit(solution)/shard_map/rk,rc->kc/dot_general | solution.py:44
  92.0 109.2 %all-gather.6.cloned.1.call-done = f32[24576,192]{0,1:T(8,128)} async-done(((f32[384,192]{0,1:T(8,128)}), f32[24576,192]{0,1:T(8,128)}) %all-gather.6.cloned.1.call-update) | async-done | bytes 18874384 | tf_op jit(solution)/shard_map/all_gather | solution.py:55
  201.2 15.6 %copy.23 = f32[24,8,64,384]{3,2,1,0:T(8,128)} copy(f32[24,8,64,384]{3,1,2,0:T(8,128)} %bitcast.33) | data formatting | bytes 37748736
  216.8 9.3 %bitcast_reduce_fusion = f32[384,192]{0,1:T(8,128)S(1)} fusion(f32[24,8,64,384]{3,2,1,0:T(8,128)} %copy.23), kind=kLoop, calls=%fused_computation.1 | loop fusion | flops 4644864 | bytes 19169280 | tf_op jit(solution)/shard_map/reduce_sum | solution.py:55
  227.7 2.6 convolution_bitcast_fusion
  230.4 4.0 %fusion.9 = f32[3072,128]{0,1:T(8,128)} fusion(f32[3072,96]{0,1:T(8,128)} %copy-done.4, f32[384,128]{1,0:T(8,128)S(1)} %copy-done.5, s32[]{:T(128)S(6)} %select_n.23), kind=kOutput, calls=%fused_computation.15 | convolution fusion | flops 452984832 | bytes 2801668 | tf_op jit(solution)/shard_map/dot_general | solution.py:49
  234.5 10.7 %reduce-scatter.10.cloned.1.call-done = f32[32,2]{1,0:T(8,128)} async-done(((f32[128,2]{1,0:T(8,128)}), f32[32,2]{1,0:T(8,128)}) %reduce-scatter.10.cloned.1.call-update) | async-done | bytes 272
  246.2 31.4 %reduce-scatter.6.cloned.1.call-done = f32[3072,32]{0,1:T(8,128)} async-done(((f32[3072,128]{0,1:T(8,128)}), f32[3072,32]{0,1:T(8,128)}) %reduce-scatter.6.cloned.1.call-update) | async-done | bytes 393232 | tf_op jit(solution)/shard_map/reduce_scatter | solution.py:51
  277.6 30.5 %reduce-scatter.8.cloned.1.call-done = f32[3072,32]{0,1:T(8,128)} async-done(((f32[3072,128]{0,1:T(8,128)}), f32[3072,32]{0,1:T(8,128)}) %reduce-scatter.8.cloned.1.call-update) | async-done | bytes 393232 | tf_op jit(solution)/shard_map/reduce_scatter | solution.py:52
  308.1 2.0 multiply_subtract_fusion
  (47 shorter events, 5.7 us)
Async XLA Ops:
  7.2 65.1 %copy-start = (f32[3072,256]{1,0:T(8,128)S(1)}, f32[3072,256]{1,0:T(8,128)}, u32[]{:S(2)}) copy-start(f32[3072,256]{1,0:T(8,128)} %param.5) | copy-start | bytes 9437188
  7.2 76.8 %all-gather.4.cloned.1.call-start = ((), (), s32[]{:S(2)}) async-start(), calls=%async_computation.5 | async-start | bytes 5898240 | tf_op jit(solution)/shard_map/all_gather | solution.py:45
  7.9 193.3 %all-gather.6.cloned.1.call-start = ((), (), s32[]{:S(2)}) async-start(), calls=%async_computation.6 | async-start | bytes 19169280 | tf_op jit(solution)/shard_map/all_gather | solution.py:55
  8.0 34.9 %collective-permute-start = (f32[3072,96]{0,1:T(8,128)}, f32[3072,96]{0,1:T(8,128)}, u32[]{:S(2)}, u32[]{:S(2)}) collective-permute-start(f32[3072,96]{0,1:T(8,128)} %param.4), channel_id=1, source_target_pairs={{0,8},{4,12},{8,16},{12,20},{16,24},{20,28},{24,32},{28,36},{32,40... | collective-permute-start | bytes 3538952 | tf_op jit(solution)/shard_map/ppermute | solution.py:9
  10.2 38.7 %collective-permute-start.1 = (f32[3072,96]{0,1:T(8,128)}, f32[3072,96]{0,1:T(8,128)}, u32[]{:S(2)}, u32[]{:S(2)}) collective-permute-start(f32[3072,96]{0,1:T(8,128)} %param.4), channel_id=1, source_target_pairs={{0,4},{4,8},{8,12},{12,16},{16,20},{20,24},{24,28},{28,32},{32,36}... | collective-permute-start | bytes 3538952 | tf_op jit(solution)/shard_map/ppermute | solution.py:9
  12.3 40.1 %collective-permute-start.2 = (f32[3072,96]{0,1:T(8,128)}, f32[3072,96]{0,1:T(8,128)}, u32[]{:S(2)}, u32[]{:S(2)}) collective-permute-start(f32[3072,96]{0,1:T(8,128)} %param.4), channel_id=1, source_target_pairs={{0,252},{4,0},{8,4},{12,8},{16,12},{20,16},{24,20},{28,24},{32,28}... | collective-permute-start | bytes 3538952 | tf_op jit(solution)/shard_map/ppermute | solution.py:9
  12.3 42.5 %collective-permute-start.3 = (f32[3072,96]{0,1:T(8,128)}, f32[3072,96]{0,1:T(8,128)}, u32[]{:S(2)}, u32[]{:S(2)}) collective-permute-start(f32[3072,96]{0,1:T(8,128)} %param.4), channel_id=1, source_target_pairs={{0,248},{4,252},{8,0},{12,4},{16,8},{20,12},{24,16},{28,20},{32,24... | collective-permute-start | bytes 3538952 | tf_op jit(solution)/shard_map/ppermute | solution.py:9
  18.7 32.6 %copy-start.2 = (f32[3072,96]{0,1:T(8,128)S(1)}, f32[3072,96]{0,1:T(8,128)}, u32[]{:S(2)}) copy-start(f32[3072,96]{0,1:T(8,128)} %param.4) | copy-start | bytes 3538948
  79.5 3.0 copy-start.3
  83.9 7.8 %copy-start.4 = (f32[3072,96]{0,1:T(8,128)}, f32[3072,96]{0,1:T(8,128)S(1)}, u32[]{:S(2)}) copy-start(f32[3072,96]{0,1:T(8,128)S(1)} %multiply_add_fusion) | copy-start | bytes 3538948
  91.7 153.5 %reduce-scatter.10.cloned.1.call-start = ((), (), s32[]{:S(2)}) async-start(), calls=%async_computation.7 | async-start | bytes 81920
  216.8 9.4 %copy-start.5 = (f32[384,128]{1,0:T(8,128)S(1)}, f32[384,128]{1,0:T(8,128)}, u32[]{:S(2)}) copy-start(f32[384,128]{1,0:T(8,128)} %param.7) | copy-start | bytes 589828
  226.2 4.1 %copy-start.7 = (f32[384,96]{0,1:T(8,128)}, f32[384,96]{0,1:T(8,128)S(1)}, u32[]{:S(2)}) copy-start(f32[384,96]{0,1:T(8,128)S(1)} %get-tuple-element.6) | copy-start | bytes 442372
  226.2 4.1 %copy-start.6 = (f32[384,96]{0,1:T(8,128)}, f32[384,96]{0,1:T(8,128)S(1)}, u32[]{:S(2)}) copy-start(f32[384,96]{0,1:T(8,128)S(1)} %get-tuple-element.5) | copy-start | bytes 442372
  227.7 50.0 %reduce-scatter.6.cloned.1.call-start = ((), (), s32[]{:S(2)}) async-start(), calls=%async_computation.3 | async-start | bytes 1966080 | tf_op jit(solution)/shard_map/reduce_scatter | solution.py:51
  230.4 79.7 %copy-start.1 = (f32[3072,256]{1,0:T(8,128)S(1)}, f32[3072,256]{1,0:T(8,128)}, u32[]{:S(2)}) copy-start(f32[3072,256]{1,0:T(8,128)} %param.5) | copy-start | bytes 9437188
  230.4 77.7 %reduce-scatter.8.cloned.1.call-start = ((), (), s32[]{:S(2)}) async-start(), calls=%async_computation.4 | async-start | bytes 1966080 | tf_op jit(solution)/shard_map/reduce_scatter | solution.py:52
  246.2 63.9 %copy-start.8 = (f32[32]{0:T(128)}, f32[32]{0:T(128)S(1)}, u32[]{:S(2)}) copy-start(f32[32]{0:T(128)S(1)} %divide_bitcast_fusion) | copy-start | bytes 388
Sparse Core Ops, SparseCore 0:
  9.8 58.6 all-gather.3
  91.8 109.2 all-gather.5
  227.8 17.3 reduce-scatter.9
  248.2 29.4 reduce-scatter.5
  280.0 28.0 reduce-scatter.7
